TPU v7x, 32 devices: a whole 2x2x4 slice. The times are simulated.
32 devices in a mesh: tm: 16 (over z, x, core), space: 2 (over y).
Axes of the slice: x: 2, y: 2, z: 4, core: 2. Of those that a mesh axis runs over, the one named last changes fastest.
Arguments:
- nodes: float32 [16, 2, 2, 8, 128, 128], P('tm', None, None, 'space'), may hold values from -3 to 3
- initial: float32 [2, 8, 128, 128], P(None, 'space'), may hold values from -3 to 3
Outputs:
- corrected: float32 [16, 2, 2, 8, 128, 128], P('tm', None, None, 'space')
All inputs are finite; a program needn't handle non-finite values.
Results may differ from a plain program's by a relative error of at most 0.0003.
Values sent between devices are 32-bit elements; how exact they have to be, the bound alone decides.
No kernel may reach another device: no remote copies, remote signals or barrier semaphores. Data moves between devices by JAX's collectives and lax.ppermute only.
A program may use at most 128 MiB of HBM per device.

v0:
```python
import math

import jax
import jax.numpy as jnp
from jax import lax
from jax.sharding import PartitionSpec as P

diffuse_fast = 0.5
diffuse_slow = 0.25
feed_rate = 0.04
kill_rate = 0.06
slice_length = 0.5
node_step = 0.25
sweep_weights = ((5.0 / 24.0, 1.0 / 3.0, -1.0 / 24.0), (-1.0 / 24.0, 1.0 / 3.0, 5.0 / 24.0))


def with_halo(x, sides, width):
    for axis, dim in sides:
        devices, length = (lax.axis_size(axis), x.shape[dim])
        up = [(i, (i + 1) % devices) for i in range(devices - 1)]
        down = [(j, i) for i, j in up]
        last = lax.slice_in_dim(x, length - width, length, axis=dim)
        leading = lax.slice_in_dim(x, 0, width, axis=dim)
        before = lax.ppermute(last, axis, up)
        after = lax.ppermute(leading, axis, down)
        x = jnp.concatenate([before, x, after], axis=dim)
    return x


def passed_along(value, axis, steps):
    count = lax.axis_size(axis)
    leading, last = (max(0, -steps), min(count, count - steps))
    return lax.ppermute(value, axis, [(source, source + steps) for source in range(leading, last)])


def entering(value, axis, join, neutral):
    count, mine = (lax.axis_size(axis), lax.axis_index(axis))
    pieces = jax.tree.map(lambda part: lax.all_gather(part, axis), value)
    subtotal = jax.tree.map(
        lambda part, zero: jnp.full_like(part, 0) + jnp.asarray(zero, part.dtype), value, neutral
    )

    def lap(position, subtotal):
        longer = join(subtotal, jax.tree.map(lambda part: part[position], pieces))
        return jax.tree.map(lambda new, old: jnp.where(position < mine, new, old), longer, subtotal)

    return lax.fori_loop(0, count - 1, lap, subtotal)


def sine_table(points, modes, stretch):
    place = jnp.arange(points).astype(jnp.float32) + 0.5
    order = jnp.arange(modes).astype(jnp.float32) + 1.0
    angle = math.pi / (stretch * modes) * place[:, None] * order[None, :]
    weight = jnp.where(jnp.arange(modes) == modes - 1, math.sqrt(0.5), 1.0).astype(jnp.float32)
    return math.sqrt(2.0 / modes) * weight[None, :] * jnp.sin(angle)


def tendency(values):
    center = values[..., 1:-1, :, :]
    padded = jnp.pad(center, [(0, 0)] * (center.ndim - 2) + [(1, 1), (1, 1)])
    laplace = (
        values[..., 2:, :, :]
        + values[..., :-2, :, :]
        + padded[..., 2:, 1:-1]
        + padded[..., :-2, 1:-1]
    )
    laplace = laplace + padded[..., 1:-1, 2:] + padded[..., 1:-1, :-2] - 6.0 * center
    first_kind = center[..., 0, :, :, :]
    second_kind = center[..., 1, :, :, :]
    reaction = (1.0 + first_kind) * second_kind * second_kind
    first_rate = diffuse_fast * laplace[..., 0, :, :, :] - reaction - feed_rate * first_kind
    second_rate = (
        diffuse_slow * laplace[..., 1, :, :, :] + reaction - (feed_rate + kill_rate) * second_kind
    )
    return jnp.stack([first_rate, second_rate], axis=-4)


def restrict(values):
    shape = values.shape
    blocks = values.reshape(shape[:-3] + (shape[-3] // 2, 2, shape[-2] // 2, 2, shape[-1] // 2, 2))
    return jnp.mean(blocks, axis=(-5, -3, -1))


def with_rims(values):
    return with_halo(values, (("space", 2),), 1)


def local(nodes, initial):
    planes_dev = initial.shape[1]
    width_x = initial.shape[2]
    width_y = initial.shape[3]
    spaces = lax.axis_size("space")
    modes_x = width_x // 2
    modes_y = width_y // 2
    modes_z = planes_dev * spaces // 2
    columns = modes_x * modes_y // spaces
    highest = lax.Precision.HIGHEST
    (w00, w01, w02), (w10, w11, w12) = sweep_weights
    own_nodes = nodes[0]
    prior_end = passed_along(own_nodes[1], "tm", 1)
    is_first = lax.axis_index("tm") == 0
    start_value = jnp.where(is_first, initial, prior_end)
    stacked = jnp.stack([start_value, own_nodes[0], own_nodes[1]])
    slopes = tendency(with_rims(stacked))
    swept_one = start_value + slice_length * (w00 * slopes[0] + w01 * slopes[1] + w02 * slopes[2])
    slope_one = tendency(with_rims(swept_one[None]))[0]
    swept_two = (
        swept_one
        + node_step * (slope_one - slopes[1])
        + slice_length * (w10 * slopes[0] + w11 * slopes[1] + w12 * slopes[2])
    )
    slope_two = tendency(with_rims(swept_two[None]))[0]
    integral_one = slice_length * (w00 * slopes[0] + w01 * slope_one + w02 * slope_two)
    integral_two = slice_length * (w10 * slopes[0] + w11 * slope_one + w12 * slope_two)
    coarse = restrict(jnp.stack([integral_one, integral_two, start_value, swept_one, swept_two]))
    forward_x = sine_table(modes_x, modes_x, 1.0).T
    forward_y = sine_table(modes_y, modes_y, 1.0).T
    forward_z = sine_table(modes_z, modes_z, 1.0).T
    along_y = jnp.einsum("by,fszxy->fszxb", forward_y, coarse, precision=highest)
    spectra_xy = jnp.einsum("ax,fszxb->fszab", forward_x, along_y, precision=highest)
    spectra_xy = spectra_xy.reshape(5, 2, planes_dev // 2, modes_x * modes_y)
    gathered = lax.all_to_all(spectra_xy, "space", split_axis=3, concat_axis=2, tiled=True)
    spectra = jnp.einsum("kz,fszc->fskc", forward_z, gathered, precision=highest)
    column_ids = lax.axis_index("space") * columns + jnp.arange(columns)
    order_x = (column_ids // modes_y + 1).astype(jnp.float32)
    order_y = (column_ids % modes_y + 1).astype(jnp.float32)
    order_z = jnp.arange(modes_z).astype(jnp.float32) + 1.0
    eigen_xy = (
        2.0 * jnp.cos(math.pi * order_x / modes_x)
        - 2.0
        + 2.0 * jnp.cos(math.pi * order_y / modes_y)
        - 2.0
    )
    eigen_z = 2.0 * jnp.cos(math.pi * order_z / modes_z) - 2.0
    eigen_sum = (eigen_z[:, None] + eigen_xy[None, :]) / 4.0
    linear = jnp.stack(
        [diffuse_fast * eigen_sum - feed_rate, diffuse_slow * eigen_sum - (feed_rate + kill_rate)]
    )
    factor = 1.0 / (1.0 - node_step * linear)
    remain_one = spectra[0] - node_step * linear * spectra[3]
    remain_two = spectra[1] - node_step * linear * spectra[4]
    seed_value = jnp.where(is_first, spectra[2], 0.0)
    element = factor * (factor * (seed_value + remain_one) + remain_two)
    log_gain = 2.0 * jnp.log(factor)

    def join_counts(earlier, later):
        return (earlier[0] + later[0], jnp.exp(later[0] * log_gain) * earlier[1] + later[1])

    _, prefix = entering(
        (jnp.ones((), jnp.float32), element),
        "tm",
        join_counts,
        (jnp.zeros((), jnp.float32), jnp.zeros_like(element)),
    )
    start_hat = jnp.where(is_first, spectra[2], prefix)
    new_one = factor * (start_hat + remain_one)
    new_two = factor * (new_one + remain_two)
    change = jnp.stack([new_one - spectra[3], new_two - spectra[4]])
    interp_x = sine_table(width_x, modes_x, 2.0)
    interp_y = sine_table(width_y, modes_y, 2.0)
    interp_z = sine_table(planes_dev * spaces, modes_z, 2.0)
    at_planes = jnp.einsum("zk,fskc->fszc", interp_z, change, precision=highest)
    returned = lax.all_to_all(at_planes, "space", split_axis=2, concat_axis=3, tiled=True)
    returned = returned.reshape(2, 2, planes_dev, modes_x, modes_y)
    widened_y = jnp.einsum("yb,fszab->fszay", interp_y, returned, precision=highest)
    refined = jnp.einsum("xa,fszay->fszxy", interp_x, widened_y, precision=highest)
    corrected = jnp.stack([swept_one + refined[0], swept_two + refined[1]])
    return corrected[None]


def solution(mesh):
    in_specs = (P("tm", None, None, "space", None, None), P(None, "space", None, None))
    out_specs = P("tm", None, None, "space", None, None)
    return jax.shard_map(local, mesh=mesh, in_specs=in_specs, out_specs=out_specs, check_vma=False)
```

profile of v0, /device:TPU:0, one launch (start us, length us, event | category | flops | bytes accessed | tf_op | source)
XLA Modules:
  0.0 521.1 jit_solution(6361830666859375832)
XLA Ops:
  14.4 6.0 %collective-permute-start.2 = (f32[3,2,1,128,128]{3,4,2,1,0:T(8,128)S(1)}, f32[3,2,1,128,128]{3,4,2,1,0:T(8,128)}, u32[]{:S(2)}, u32[]{:S(2)}) collective-permute-start(f32[3,2,1,128,128]{3,4,2,1,0:T(8,128)S(1)} %get-tuple-element.157), channel_id=1, source_target_pairs={{0,1},{2,3},{4,5},{6,7},{8,9},{10,11},{12,13},{14,15},{16,17},{18,... | collective-permute-start | bytes 1179656 | tf_op jit(solution)/shard_map/ppermute | solution.py:24
  28.9 4.6 collective-permute-start.4
  38.6 5.1 collective-permute-start.6
  43.7 34.9 %reshape.454 = f32[1,2,2,2,64,2,64,2]{5,4,7,6,3,2,1,0:T(8,128)} reshape(f32[2,4,128,128]{2,3,1,0:T(8,128)S(1)} %broadcast_select_fusion) | data formatting | bytes 1048576 | tf_op jit(solution)/shard_map/stack | solution.py:115
  78.6 22.8 %copy.49 = f32[1,2,2,2,64,2,64,2]{6,4,7,5,3,2,1,0:T(8,128)S(1)} copy(f32[1,2,2,2,64,2,64,2]{5,4,7,6,3,2,1,0:T(8,128)} %reshape.454) | data formatting | bytes 1048576 | tf_op jit(solution)/shard_map/stack | solution.py:115
  101.4 34.8 %reshape.455 = f32[1,2,2,2,64,2,64,2]{5,4,7,6,3,2,1,0:T(8,128)} reshape(f32[2,4,128,128]{2,3,1,0:T(8,128)S(1)} %get-tuple-element.150) | data formatting | bytes 1048576 | tf_op jit(solution)/shard_map/stack | solution.py:115
  136.3 23.8 %copy.50 = f32[1,2,2,2,64,2,64,2]{6,4,7,5,3,2,1,0:T(8,128)} copy(f32[1,2,2,2,64,2,64,2]{5,4,7,6,3,2,1,0:T(8,128)} %reshape.455) | data formatting | bytes 1048576 | tf_op jit(solution)/shard_map/stack | solution.py:115
  160.0 34.8 %reshape.456 = f32[1,2,2,2,64,2,64,2]{5,4,7,6,3,2,1,0:T(8,128)} reshape(f32[2,4,128,128]{2,3,1,0:T(8,128)S(1)} %bitcast_add_fusion.1) | data formatting | bytes 1048576 | tf_op jit(solution)/shard_map/stack | solution.py:115
  194.9 23.8 %copy.51 = f32[1,2,2,2,64,2,64,2]{6,4,7,5,3,2,1,0:T(8,128)} copy(f32[1,2,2,2,64,2,64,2]{5,4,7,6,3,2,1,0:T(8,128)} %reshape.456) | data formatting | bytes 1048576 | tf_op jit(solution)/shard_map/stack | solution.py:115
  220.3 35.6 %reshape.452 = f32[1,2,2,2,64,2,64,2]{5,4,7,6,3,2,1,0:T(8,128)} reshape(f32[1,2,4,128,128]{3,4,2,1,0:T(8,128)} %get-tuple-element.155) | data formatting | bytes 1048576 | tf_op jit(solution)/shard_map/stack | solution.py:115
  255.9 23.8 %copy.47 = f32[1,2,2,2,64,2,64,2]{6,4,7,5,3,2,1,0:T(8,128)} copy(f32[1,2,2,2,64,2,64,2]{5,4,7,6,3,2,1,0:T(8,128)} %reshape.452) | data formatting | bytes 1048576 | tf_op jit(solution)/shard_map/stack | solution.py:115
  282.1 34.8 %reshape.453 = f32[1,2,2,2,64,2,64,2]{5,4,7,6,3,2,1,0:T(8,128)} reshape(f32[1,2,4,128,128]{3,4,2,1,0:T(8,128)S(1)} %copy-done.2) | data formatting | bytes 1048576 | tf_op jit(solution)/shard_map/stack | solution.py:115
  316.9 23.9 %copy.48 = f32[1,2,2,2,64,2,64,2]{6,4,7,5,3,2,1,0:T(8,128)} copy(f32[1,2,2,2,64,2,64,2]{5,4,7,6,3,2,1,0:T(8,128)} %reshape.453) | data formatting | bytes 1048576 | tf_op jit(solution)/shard_map/stack | solution.py:115
  353.7 9.3 %copy.74 = f32[5,2,2,64,64]{0,2,1,4,3:T(2,128)} copy(f32[5,2,2,64,64]{3,4,2,1,0:T(8,128)S(1)} %convolution_bitcast_fusion.3) | data formatting | bytes 655360 | tf_op jit(solution)/shard_map/reshape | solution.py:121
  363.0 15.4 %reshape.457 = f32[2,1,40960]{2,1,0:T(1,128)} reshape(f32[4096,2,2,5]{3,2,1,0:T(2,128)} %bitcast.154) | data formatting | bytes 655360
  378.4 3.5 all-to-all-start
  382.1 5.2 %all-to-all-done = f32[2,1,40960]{2,1,0:T(1,128)S(1)} async-done(((f32[2,1,40960]{2,1,0:T(1,128)}), f32[2,1,40960]{2,1,0:T(1,128)S(1)}, u32[]{:S(2)}, u32[]{:S(2)}) %all-to-all-start) | async-done | bytes 327712 | tf_op jit(solution)/shard_map/all_to_all | solution.py:122
  389.5 15.5 %reshape.458 = f32[4096,2,2,5]{3,2,1,0:T(2,128)} reshape(f32[2,40960]{1,0:T(2,128)S(1)} %reduce) | data formatting | bytes 655360
  405.0 10.3 %copy.55 = f32[5,2,2,2,2048]{4,2,3,1,0:T(2,128)S(1)} copy(f32[5,2,2,2,2048]{0,2,1,4,3:T(2,128)} %bitcast.155) | data formatting | bytes 655360 | tf_op jit(solution)/shard_map/all_to_all | solution.py:122
  418.5 39.5 %all-reduce.3 = f32[16]{0:T(128)S(1)} all-reduce(f32[16]{0:T(128)S(1)} %dynamic-update-slice), channel_id=1, replica_groups=mesh['tm'=16,'space'=2] {'tm'}, use_global_device_ids=true, to_apply=%add.3 | all-reduce | flops 16 | bytes 128
  458.0 7.7 %all-gather.2.cloned.1.call-done = f32[16,2,4,2048]{3,2,1,0:T(4,128)} async-done(((f32[1,2,4,2048]{3,2,1,0:T(4,128)}), f32[16,2,4,2048]{3,2,1,0:T(4,128)}) %all-gather.2.cloned.1.call-update) | async-done | bytes 1048592 | tf_op jit(solution)/shard_map/all_gather | solution.py:38
  465.7 32.5 %while.14 = (s32[]{:T(128)}, f32[2,4,2048]{2,1,0:T(4,128)S(1)}, s32[]{:T(128)}, f32[16]{0:T(128)S(1)}, f32[2,4,2048]{2,1,0:T(4,128)S(1)}, /*index=5*/f32[16,2,4,2048]{3,2,1,0:T(4,128)}, s32[]{:T(128)}, s32[]{:T(128)}) while((s32[]{:T(128)}, f32[2,4,2048]{2,1,0:T(4,128)S(1)}, s32[]{:T(128)}, f32[16]{0:T(128)S(1)}, ...), condition=%wide.region_2.3_spmd.clone, body=%wide.region_1.2_spmd.clone.sunk | while | flops 81924 | bytes 262269 | solution.py:47
  499.8 3.7 all-to-all-start.1
  503.5 5.8 %all-to-all-done.1 = f32[2,2,8,2048]{3,1,0,2:T(2,128)S(1)} async-done(((f32[2,2,8,2048]{3,1,0,2:T(2,128)}), f32[2,2,8,2048]{3,1,0,2:T(2,128)S(1)}, u32[]{:S(2)}, u32[]{:S(2)}) %all-to-all-start.1) | async-done | bytes 262176 | tf_op jit(solution)/shard_map/all_to_all | solution.py:163
  (109 shorter events, 82.5 us)
Async XLA Ops:
  6.5 4.8 copy-start.3
  8.1 4.1 collective-permute-start
  13.2 10.0 %collective-permute-start.1 = (f32[3,2,1,128,128]{3,4,2,1,0:T(8,128)}, f32[3,2,1,128,128]{3,4,2,1,0:T(8,128)}, u32[]{:S(2)}, u32[]{:S(2)}) collective-permute-start(f32[3,2,1,128,128]{3,4,2,1,0:T(8,128)} %get-tuple-element.156), channel_id=1, source_target_pairs={{1,0},{3,2},{5,4},{7,6},{9,8},{11,10},{13,12},{15,14},{17,16},{19,... | collective-permute-start | bytes 1179656 | tf_op jit(solution)/shard_map/ppermute | solution.py:25
  14.4 10.6 %collective-permute-start.2 = (f32[3,2,1,128,128]{3,4,2,1,0:T(8,128)S(1)}, f32[3,2,1,128,128]{3,4,2,1,0:T(8,128)}, u32[]{:S(2)}, u32[]{:S(2)}) collective-permute-start(f32[3,2,1,128,128]{3,4,2,1,0:T(8,128)S(1)} %get-tuple-element.157), channel_id=1, source_target_pairs={{0,1},{2,3},{4,5},{6,7},{8,9},{10,11},{12,13},{14,15},{16,17},{18,... | collective-permute-start | bytes 1179656 | tf_op jit(solution)/shard_map/ppermute | solution.py:24
  27.6 6.9 %collective-permute-start.3 = (f32[1,2,1,128,128]{3,4,2,1,0:T(8,128)S(1)}, f32[1,2,1,128,128]{3,4,2,1,0:T(8,128)S(1)}, u32[]{:S(2)}, u32[]{:S(2)}) collective-permute-start(f32[1,2,1,128,128]{3,4,2,1,0:T(8,128)S(1)} %get-tuple-element.168), channel_id=1, source_target_pairs={{1,0},{3,2},{5,4},{7,6},{9,8},{11,10},{13,12},{15,14},{17,16},{19,... | collective-permute-start | bytes 393224 | tf_op jit(solution)/shard_map/ppermute | solution.py:25
  28.9 7.1 %collective-permute-start.4 = (f32[1,2,1,128,128]{3,4,2,1,0:T(8,128)S(1)}, f32[1,2,1,128,128]{3,4,2,1,0:T(8,128)S(1)}, u32[]{:S(2)}, u32[]{:S(2)}) collective-permute-start(f32[1,2,1,128,128]{3,4,2,1,0:T(8,128)S(1)} %get-tuple-element.169), channel_id=1, source_target_pairs={{0,1},{2,3},{4,5},{6,7},{8,9},{10,11},{12,13},{14,15},{16,17},{18,... | collective-permute-start | bytes 393224 | tf_op jit(solution)/shard_map/ppermute | solution.py:24
  37.3 181.3 %collective-permute-start.5 = (f32[1,2,1,128,128]{3,4,2,1,0:T(8,128)}, f32[1,2,1,128,128]{3,4,2,1,0:T(8,128)S(1)}, u32[]{:S(2)}, u32[]{:S(2)}) collective-permute-start(f32[1,2,1,128,128]{3,4,2,1,0:T(8,128)} %get-tuple-element.166), channel_id=1, source_target_pairs={{1,0},{3,2},{5,4},{7,6},{9,8},{11,10},{13,12},{15,14},{17,16},{19,... | collective-permute-start | bytes 393224 | tf_op jit(solution)/shard_map/ppermute | solution.py:25
  38.6 180.0 %collective-permute-start.6 = (f32[1,2,1,128,128]{3,4,2,1,0:T(8,128)}, f32[1,2,1,128,128]{3,4,2,1,0:T(8,128)S(1)}, u32[]{:S(2)}, u32[]{:S(2)}) collective-permute-start(f32[1,2,1,128,128]{3,4,2,1,0:T(8,128)} %get-tuple-element.167), channel_id=1, source_target_pairs={{0,1},{2,3},{4,5},{6,7},{8,9},{10,11},{12,13},{14,15},{16,17},{18,... | collective-permute-start | bytes 393224 | tf_op jit(solution)/shard_map/ppermute | solution.py:24
  279.7 2.4 copy-start.2
  343.1 1.6 copy-start
  344.8 1.6 copy-start.1
  378.4 9.0 %all-to-all-start = ((f32[2,1,40960]{2,1,0:T(1,128)}), f32[2,1,40960]{2,1,0:T(1,128)S(1)}, u32[]{:S(2)}, u32[]{:S(2)}) async-start(f32[2,1,40960]{2,1,0:T(1,128)} %reshape.457), calls=%async_computation | async-start | bytes 655360 | tf_op jit(solution)/shard_map/all_to_all | solution.py:122
  381.9 83.8 %all-gather.2.cloned.1.call-start = ((), (), s32[]{:S(2)}) async-start(), calls=%async_computation.2 | async-start | bytes 1114112 | tf_op jit(solution)/shard_map/all_gather | solution.py:38
  415.3 1.8 copy-start.4
  499.8 9.5 %all-to-all-start.1 = ((f32[2,2,8,2048]{3,1,0,2:T(2,128)}), f32[2,2,8,2048]{3,1,0,2:T(2,128)S(1)}, u32[]{:S(2)}, u32[]{:S(2)}) async-start(f32[2,2,8,2048]{3,1,0,2:T(2,128)} %copy.56), calls=%async_computation.1 | async-start | bytes 524288 | tf_op jit(solution)/shard_map/all_to_all | solution.py:163
Sparse Core Ops, SparseCore 0:
  417.2 48.3 all-gather.1
where the time goes:
time: 528 us; the launch traced here: 521 us
  local copies, waits for them, and re-layouts  370 us (70%)
  blocking collectives  39.5 us (7%)
  other arithmetic  34.8 us (7%)
  starting transfers between devices  30.1 us (6%)
  waiting for transfers between devices  25.9 us (5%)
  between operations  14 us (3%)
  matrix products  6.93 us (1%)
    another operation x11, local copies, waits for them, and re-layouts, local(): jnp.stack([integral_one, integral_two, start_value, swept_one, swept_two])  294 us
    unnamed x22, local copies, waits for them, and re-layouts  40.7 us
    unnamed x1, blocking collectives  39.5 us
    select_n x15, other arithmetic, lap(): jnp.where(position < mine, new, old)  23.6 us
    ppermute x3, starting transfers between devices, with_halo(): before = lax.ppermute(last, axis, up)  15.7 us
    all_to_all x3, local copies, waits for them, and re-layouts, local(): lax.all_to_all(spectra_xy, 'space', split_axis=3, concat_axis=2, tiled=True)  11.1 us
  transfers between devices with their start and end apart: 10, of which 8 were waited for; matrix products, arithmetic and copies ran while one was open for 34% of the time, Pallas kernels for 0%

commit v1 on v0

v1 whole, which is shorter than its diff:
```python
import functools
import math

import jax
import jax.numpy as jnp
import numpy as np
from jax import lax
from jax.experimental import pallas as pl
from jax.experimental.pallas import tpu as pltpu
from jax.sharding import PartitionSpec as P

diffusion = (0.5, 0.25)
feed_rate = 0.04
kill_rate = 0.06
decay = (feed_rate, feed_rate + kill_rate)
slice_length = 0.5
node_step = 0.25
sweep_weights = ((5.0 / 24.0, 1.0 / 3.0, -1.0 / 24.0), (-1.0 / 24.0, 1.0 / 3.0, 5.0 / 24.0))
(T00, T01, T02), (T10, T11, T12) = [[slice_length * w for w in row] for row in sweep_weights]
AXES = ("tm", "space")


def sine_table(points, modes):
    place = np.arange(points) + 0.5
    order = np.arange(modes) + 1.0
    weight = np.where(np.arange(modes) == modes - 1, math.sqrt(0.5), 1.0)
    return math.sqrt(2.0 / modes) * weight[None, :] * np.sin(math.pi / points * place[:, None] * order[None, :])


def split(table):
    table = jnp.asarray(table, jnp.float32)
    high = table.astype(jnp.bfloat16)
    low = (table - high.astype(jnp.float32)).astype(jnp.bfloat16)
    return high, low


def np_split(table):
    table = np.asarray(table, np.float32)
    high = table.astype(jnp.bfloat16)
    low = (table - high.astype(np.float32)).astype(jnp.bfloat16)
    return high, low


def restricted(modes):
    return np.repeat(sine_table(modes, modes).T, 2, axis=1) * 0.5


def doubled(table):
    rows, columns = table.shape
    both = np.zeros((2 * rows, 2 * columns))
    both[:rows, :columns] = table
    both[rows:, columns:] = table
    return both


def eigen(count):
    return 2.0 * np.cos(math.pi * (np.arange(count) + 1.0) / count) - 2.0


def factor_table(modes_z, modes_x, modes_y):
    total = (eigen(modes_z)[:, None, None] + eigen(modes_x)[None, :, None] + eigen(modes_y)[None, None, :]) / 4.0
    linear = np.stack([diffusion[i] * total - decay[i] for i in range(2)], axis=2)
    factor = 1.0 / (1.0 - node_step * linear)
    return np.asarray(factor.reshape(modes_z * modes_x, 2 * modes_y), np.float32)


def in_plane(v):
    rows, lanes = v.shape
    row = lax.broadcasted_iota(jnp.int32, v.shape, 0)
    lane = lax.broadcasted_iota(jnp.int32, v.shape, 1)
    up = jnp.where(row == rows - 1, 0.0, pltpu.roll(v, rows - 1, 0))
    down = jnp.where(row == 0, 0.0, pltpu.roll(v, 1, 0))
    left = jnp.where(lane == lanes - 1, 0.0, pltpu.roll(v, lanes - 1, 1))
    right = jnp.where(lane == 0, 0.0, pltpu.roll(v, 1, 1))
    return (up + down) + (left + right)


def slopes(p, q, beside_p, beside_q):
    lap_p = in_plane(p) + beside_p - 6.0 * p
    lap_q = in_plane(q) + beside_q - 6.0 * q
    reaction = (1.0 + p) * q * q
    return (
        diffusion[0] * lap_p - reaction - decay[0] * p,
        diffusion[1] * lap_q + reaction - decay[1] * q,
    )


def dot(a, b):
    return jnp.dot(a, b, preferred_element_type=jnp.float32)


def edge_plane(side, planes, inward):
    if isinstance(side, int):
        return inward if side == 0 else planes - 1 - inward
    return jnp.where(side == 0, inward, planes - 1 - inward)


def facing(spaces):
    if spaces == 2:
        return [1 - lax.axis_index("space")]
    return [0, 1]


def prepare_kernel(spaces, count, nodes, initial, finish, *outs):
    planes = nodes.shape[3]
    is_last = lax.axis_index("tm") == count - 1
    finish[...] = nodes[0, 1]
    for n, side in enumerate(facing(spaces)):
        own, diagonal = outs[2 * n], outs[2 * n + 1]
        first, second = edge_plane(side, planes, 0), edge_plane(side, planes, 1)

        def at(node, plane):
            return [nodes[0, node, s, plane] for s in range(2)]

        mid, end = at(0, first), at(1, first)
        mid_slope = slopes(*mid, *at(0, second))
        end_slope = slopes(*end, *at(1, second))
        start = [jnp.where(is_last, initial[s, first], end[s]) for s in range(2)]
        beside = [jnp.where(is_last, initial[s, second], nodes[0, 1, s, second]) for s in range(2)]
        start_slope = slopes(*start, *beside)
        for s in range(2):
            own[0, s] = T01 * mid[s] + T02 * end[s]
            own[1, s] = (
                node_step * (T01 * mid_slope[s] + T02 * end_slope[s])
                + (T11 - node_step) * mid[s]
                + T12 * end[s]
            )
            diagonal[0, s] = start[s]
            diagonal[1, s] = node_step * (start[s] + T00 * start_slope[s]) + T10 * start[s]


def sweep_kernel(spaces, *refs):
    refs = list(refs)
    table_z, interp_z = refs.pop(0), refs.pop(0)
    nodes, initial, prior = refs.pop(0), refs.pop(0), refs.pop(0)
    halos = [(refs.pop(0), refs.pop(0)) for _ in range(1 if spaces == 2 else 2)]
    table_x, table_y, table_f = refs.pop(0), refs.pop(0), refs.pop(0)
    swept, element, keep = refs.pop(0), refs.pop(0), refs.pop(0)
    sends = [refs.pop(0) for _ in range(spaces - 1)]
    start, slope0, rest, xs, ys, stack, spec = refs
    planes = nodes.shape[3]
    half = planes // 2
    modes_x = table_x.shape[1]
    modes_z = table_f.shape[0] // modes_x
    lanes = table_f.shape[1]
    me = lax.axis_index("space")
    is_first = lax.axis_index("tm") == 0
    sides = facing(spaces)

    def beside(get, plane):
        around = [get(z) for z in (plane - 1, plane + 1) if 0 <= z < planes]
        return around[0] if len(around) == 1 else around[0] + around[1]

    def slope_of(ref, plane):
        args = [ref[s, plane] for s in range(2)] + [beside(lambda z: ref[s, z], plane) for s in range(2)]
        return slopes(*args)

    for z in range(planes):
        for s in range(2):
            start[s, z] = jnp.where(is_first, initial[s, z], prior[s, z])
    middle, finish = nodes.at[0, 0], nodes.at[0, 1]
    one, two = swept.at[0], swept.at[1]
    for z in range(planes):
        f0, f1, f2 = slope_of(start, z), slope_of(middle, z), slope_of(finish, z)
        for s in range(2):
            one[s, z] = start[s, z] + T00 * f0[s] + T01 * f1[s] + T02 * f2[s]
            rest[s, z] = T10 * f0[s] + (T11 - node_step) * f1[s] + T12 * f2[s]
            slope0[s, z] = f0[s]
    for side, (own, diagonal) in zip(sides, halos):
        edge = edge_plane(side, planes, 0)
        for s in range(2):
            d = diffusion[s]
            one[s, edge] = one[s, edge] + d * (T00 * diagonal[0, s] + own[0, s])
            back = T00 * start[s, edge] + T01 * middle[s, edge] + T02 * finish[s, edge]
            if spaces != 2:
                back = jnp.where(me == (0 if side == 0 else spaces - 1), 0.0, back)
            rest[s, edge] = rest[s, edge] + d * (own[1, s] + diagonal[1, s] + (node_step * d) * back)
    for z in range(planes):
        g1 = slope_of(one, z)
        for s in range(2):
            first = one[s, z]
            second = first + node_step * g1[s] + rest[s, z]
            two[s, z] = second
            x = T00 * slope0[s, z] + T01 * g1[s] - first
            xs[s, z] = x + jnp.where(is_first, start[s, z], 0.0)
            ys[s, z] = T10 * slope0[s, z] + T11 * g1[s] + first - second
    width_y = nodes.shape[5]
    rows = nodes.shape[4]

    def put(slot, s, value):
        stack[pl.ds(slot * rows, rows), pl.ds(s * width_y, width_y)] = value

    for c in range(half):
        pair = [slope_of(two, 2 * c), slope_of(two, 2 * c + 1)]
        for s in range(2):
            g2 = pair[0][s] + pair[1][s]
            put(c, s, 0.5 * (xs[s, 2 * c] + xs[s, 2 * c + 1] + T02 * g2))
            put(half + c, s, 0.5 * (ys[s, 2 * c] + ys[s, 2 * c + 1] + T12 * g2))
            put(2 * half + c, s, 0.5 * (two[s, 2 * c] + two[s, 2 * c + 1]))
    for n, side in enumerate(sides):
        edge = edge_plane(side, planes, 0)
        for s in range(2):
            d = 0.5 * diffusion[s]
            put(3 * half + 2 * n, s, d * (T00 * start[s, edge] + T01 * one[s, edge] + T02 * two[s, edge]))
            put(3 * half + 2 * n + 1, s, d * (T10 * start[s, edge] + T11 * one[s, edge] + T12 * two[s, edge]))
    fields = 3 * half + 2 * len(sides)
    y_high, y_low = table_y[0], table_y[1]
    x_high, x_low = table_x[0], table_x[1]
    for f in range(fields):
        high, low = split(stack[pl.ds(f * rows, rows), :])
        along_y = dot(high, y_high) + (dot(low, y_high) + dot(high, y_low))
        high, low = split(along_y)
        spec[f] = dot(x_high, high) + (dot(x_low, high) + dot(x_high, low))

    x_parts, y_parts = [], []
    for k in range(modes_z):
        factor = table_f[pl.ds(k * modes_x, modes_x), :]
        weights = [table_z[k, me * half + c] for c in range(half)]
        x = sum(weights[c] * spec[c] for c in range(half))
        y = sum(weights[c] * spec[half + c] for c in range(half))
        e = sum(weights[c] * spec[2 * half + c] for c in range(half))
        for n, side in enumerate(sides):
            beyond = me * half + jnp.where(side == 0, -1, half)
            inside = (beyond >= 0) & (beyond < spaces * half)
            weight = jnp.where(inside, table_z[k, jnp.clip(beyond, 0, spaces * half - 1)], 0.0)
            x = x + weight * spec[3 * half + 2 * n]
            y = y + weight * spec[3 * half + 2 * n + 1]
        x = factor * x
        y = factor * (x + y)
        element[pl.ds(k * modes_x, modes_x), :] = y + e
        x_parts.append(x)
        y_parts.append(y)
    for j, target in enumerate([keep] + sends):
        device = lax.rem(me + j, spaces)
        for z in range(planes):
            place = device * planes + z
            weights = [interp_z[place, k] for k in range(modes_z)]
            target[0, z] = sum(w * v for w, v in zip(weights, x_parts))
            target[1, z] = sum(w * v for w, v in zip(weights, y_parts))


def chain_kernel(count, spaces, pieces, factor, out):
    gain = factor[...] * factor[...]
    state = jnp.zeros_like(gain)
    for t in range(count):
        for s in range(spaces):
            out[t * spaces + s] = state
        if t < count - 1:
            total = pieces[t * spaces]
            for s in range(1, spaces):
                total = total + pieces[t * spaces + s]
            state = gain * state + total


def finish_kernel(spaces, interp_z, carried, swept, keep, *refs):
    received = refs[: spaces - 1]
    table_x, table_y, table_f, out, left, right = refs[spaces - 1 :]
    planes = keep.shape[1]
    modes_x = keep.shape[2]
    modes_z = table_f.shape[0] // modes_x
    width_y = out.shape[5]
    me = lax.axis_index("space")
    for k in range(modes_z):
        part = pl.ds(k * modes_x, modes_x)
        left[part, :] = table_f[part, :] * carried[part, :]
        right[part, :] = table_f[part, :] * left[part, :]
    y_high, y_low = table_y[0], table_y[1]
    x_high, x_low = table_x[0], table_x[1]
    for node, source in ((0, left), (1, right)):
        for z in range(planes):
            value = keep[node, z]
            for other in received:
                value = value + other[node, z]
            for k in range(modes_z):
                weight = interp_z[me * planes + z, k]
                value = value + weight * source[pl.ds(k * modes_x, modes_x), :]
            high, low = split(value)
            wide = dot(high, y_high) + (dot(low, y_high) + dot(high, y_low))
            high, low = split(wide)
            fine = dot(x_high, high) + (dot(x_low, high) + dot(x_high, low))
            for s in range(2):
                out[0, node, s, z] = swept[node, s, z] + fine[:, s * width_y : (s + 1) * width_y]


def local(nodes, initial):
    count, spaces = lax.axis_size("tm"), lax.axis_size("space")
    planes, width_x, width_y = initial.shape[1:]
    modes_x, modes_y, modes_z = width_x // 2, width_y // 2, planes * spaces // 2
    half, lanes = planes // 2, 2 * modes_y
    devices = count * spaces
    f32 = jnp.float32
    shape = jax.ShapeDtypeStruct
    vmem, smem = pl.BlockSpec(memory_space=pltpu.VMEM), pl.BlockSpec(memory_space=pltpu.SMEM)
    params = pltpu.CompilerParams(vmem_limit_bytes=24 << 20)
    sides = 1 if spaces == 2 else 2

    forward_z = jnp.asarray(sine_table(modes_z, modes_z).T, f32)
    interp_z = jnp.asarray(sine_table(planes * spaces, modes_z), f32)
    forward_x = jnp.stack([jnp.asarray(t) for t in np_split(restricted(modes_x))])
    forward_y = jnp.stack([jnp.asarray(t) for t in np_split(doubled(restricted(modes_y).T))])
    interp_x = jnp.stack([jnp.asarray(t) for t in np_split(sine_table(width_x, modes_x))])
    interp_y = jnp.stack([jnp.asarray(t) for t in np_split(doubled(sine_table(width_y, modes_y).T))])
    factors = jnp.asarray(factor_table(modes_z, modes_x, modes_y))

    plane_pair = shape((2, 2, width_x, width_y), f32)
    prepared = pl.pallas_call(
        functools.partial(prepare_kernel, spaces, count),
        out_shape=[shape((2, planes, width_x, width_y), f32)] + [plane_pair] * (2 * sides),
        in_specs=[vmem, vmem],
        out_specs=[vmem] * (1 + 2 * sides),
        compiler_params=params,
        name="prepare",
    )(nodes, initial)
    finish = prepared[0]
    prior = lax.ppermute(finish, "tm", [(t, t + 1) for t in range(count - 1)])
    halos = []
    for n in range(sides):
        if spaces == 2:
            moves = [(0, 1), (1, 0)]
        else:
            step = -1 if n == 0 else 1
            moves = [(s, s + step) for s in range(spaces) if 0 <= s + step < spaces]
        across = [(t * spaces + a, (t + 1) % count * spaces + b) for t in range(count) for a, b in moves]
        own = lax.ppermute(prepared[1 + 2 * n], "space", moves)
        diagonal = lax.ppermute(prepared[2 + 2 * n], AXES, across)
        halos.append((own, diagonal))
    if spaces != 2:
        halos = halos[::-1]
    halo_args = [value for pair in halos for value in pair]

    rows = modes_z * modes_x
    block = shape((2, planes, modes_x, lanes), f32)
    fields = 3 * half + 2 * sides
    whole = pltpu.VMEM((2, planes, width_x, width_y), f32)
    results = pl.pallas_call(
        functools.partial(sweep_kernel, spaces),
        out_shape=[shape((2, 2, planes, width_x, width_y), f32), shape((rows, lanes), f32)] + [block] * spaces,
        in_specs=[smem, smem] + [vmem] * (3 + 2 * sides + 3),
        out_specs=[vmem] * (2 + spaces),
        scratch_shapes=[whole] * 5
        + [pltpu.VMEM((fields * width_x, 2 * width_y), f32), pltpu.VMEM((fields, modes_x, lanes), f32)],
        compiler_params=params,
        name="sweep",
    )(forward_z, interp_z, nodes, initial, prior, *halo_args, forward_x, forward_y, factors)
    swept, element, keep, sends = results[0], results[1], results[2], results[3:]

    share = rows // devices
    pieces = lax.all_to_all(element.reshape(devices, share, lanes), AXES, 0, 0, tiled=True)
    received = [
        lax.ppermute(send, "space", [(s, (s + j) % spaces) for s in range(spaces)])
        for j, send in enumerate(sends, 1)
    ]
    place = lax.axis_index(AXES) * share
    own_factor = lax.dynamic_slice_in_dim(factors, place, share, axis=0)
    carried = pl.pallas_call(
        functools.partial(chain_kernel, count, spaces),
        out_shape=shape((devices, share, lanes), f32),
        in_specs=[vmem, vmem],
        out_specs=vmem,
        compiler_params=params,
        name="chain",
    )(pieces, own_factor)
    carried = lax.all_to_all(carried, AXES, 0, 0, tiled=True).reshape(rows, lanes)

    return pl.pallas_call(
        functools.partial(finish_kernel, spaces),
        out_shape=shape((1, 2, 2, planes, width_x, width_y), f32),
        in_specs=[smem] + [vmem] * (3 + spaces - 1 + 3),
        out_specs=vmem,
        scratch_shapes=[pltpu.VMEM((rows, lanes), f32)] * 2,
        compiler_params=params,
        name="finish",
    )(interp_z, carried, swept, keep, *received, interp_x, interp_y, factors)


def solution(mesh):
    in_specs = (P("tm", None, None, "space", None, None), P(None, "space", None, None))
    out_specs = P("tm", None, None, "space", None, None)
    return jax.shard_map(local, mesh=mesh, in_specs=in_specs, out_specs=out_specs, check_vma=False)
```

time: 528 us -> 54.5 us (0.10); the launches traced: 521 us -> 54.2 us
  local copies, waits for them, and re-layouts: 370 us -> 2.3 us
  blocking collectives: 39.5 us -> 0 us
  other arithmetic: 34.8 us -> 0 us
  between operations: 14 us -> 0.09 us
  starting transfers between devices: 30.1 us -> 16.4 us
  Pallas kernels: 0 us -> 9.35 us
  matrix products: 6.93 us -> 0 us
    another operation x11 -> x0, local copies, waits for them, and re-layouts: 294 us -> none  [local(): jnp.stack([integral_one, integral_two, start_value, swept_one, swept_two])]
    unnamed x1 -> x0, blocking collectives: 39.5 us -> none
    unnamed x22 -> x18, local copies, waits for them, and re-layouts: 40.7 us -> 2.29 us
    select_n x16 -> x0, other arithmetic: 23.6 us -> none  [the longest x15 23.6 us: lap(): jnp.where(position < mine, new, old)]
    ppermute x7 -> x4, starting transfers between devices: 22.7 us -> 8.24 us  [the longest x1 2.43 us: local(): prior = lax.ppermute(finish, 'tm', [(t, t + 1) for t in range(count - 1)])]
    all_to_all x4 -> x0, local copies, waits for them, and re-layouts: 11.3 us -> none  [the longest x3 11.1 us: local(): lax.all_to_all(spectra_xy, 'space', split_axis=3, concat_axis=2, tiled=True)]
    reshape x2 -> x0, local copies, waits for them, and re-layouts: 9.61 us -> none  [the longest x1 9.27 us: local(): spectra_xy = spectra_xy.reshape(5, 2, planes_dev // 2, modes_x * modes_y)]
    pallas_call x0 -> x4, Pallas kernels: none -> 9.35 us  [the longest x1 5.25 us: local(): pl.pallas_call(functools.partial(sweep_kernel, spaces), out_shape=[shape(...]
  transfers between devices with their start and end apart: 10 -> 6, of which waited for: 8 -> 4; matrix products, arithmetic and copies ran while one was open for 34% -> 0% of each run, Pallas kernels for 0% -> 1%
where the time goes in v1:
time: 54.5 us; the launch traced here: 54.2 us
  waiting for transfers between devices  26.1 us (48%)
  starting transfers between devices  16.4 us (30%)
  Pallas kernels  9.35 us (17%)
  local copies, waits for them, and re-layouts  2.3 us (4%)
    all_to_all x1, waiting for transfers between devices, local(): lax.all_to_all(carried, AXES, 0, 0, tiled=True).reshape(rows, lanes)  8.59 us
    ppermute x1, waiting for transfers between devices, local(): own = lax.ppermute(prepared[1 + 2 * n], 'space', moves)  7.16 us
    all_to_all x1, waiting for transfers between devices, local(): lax.all_to_all(element.reshape(devices, share, lanes), AXES, 0, 0, tiled=...  6.76 us
    all_to_all x1, starting transfers between devices, local(): lax.all_to_all(element.reshape(devices, share, lanes), AXES, 0, 0, tiled=...  5.42 us
    pallas_call x1, Pallas kernels, local(): pl.pallas_call(functools.partial(sweep_kernel, spaces), out_shape=[shape(...  5.25 us
    ppermute x1, waiting for transfers between devices, local(): diagonal = lax.ppermute(prepared[2 + 2 * n], AXES, across)  3.58 us
    pallas_call x1, Pallas kernels, local(): pl.pallas_call(functools.partial(finish_kernel, spaces), out_shape=shape(...  3.02 us
    all_to_all x1, starting transfers between devices, local(): lax.all_to_all(carried, AXES, 0, 0, tiled=True).reshape(rows, lanes)  2.71 us
  transfers between devices with their start and end apart: 6, of which 4 were waited for; matrix products, arithmetic and copies ran while one was open for 0% of the time, Pallas kernels for 1%

profile of v1, /device:TPU:0, one launch (start us, length us, event | category | flops | bytes accessed | tf_op | source)
XLA Modules:
  0.0 54.2 jit_solution(14220125242478365332)
XLA Ops:
  0.0 1.2 %copy-done = f32[1,2,2,4,128,128]{5,4,3,2,1,0:T(8,128)S(1)} copy-done((f32[1,2,2,4,128,128]{5,4,3,2,1,0:T(8,128)S(1)}, f32[1,2,2,4,128,128]{5,4,3,2,1,0:T(8,128)}, u32[]{:S(2)}) %copy-start) | copy-done | bytes 1048600
  1.2 1.0 %copy-done.1 = f32[2,4,128,128]{3,2,1,0:T(8,128)S(1)} copy-done((f32[2,4,128,128]{3,2,1,0:T(8,128)S(1)}, f32[2,4,128,128]{3,2,1,0:T(8,128)}, u32[]{:S(2)}) %copy-start.1) | copy-done | bytes 524312
  2.3 0.4 prepare.1
  2.7 0.0 copy-start.7
  2.7 2.4 %collective-permute-start = (f32[2,4,128,128]{3,2,1,0:T(8,128)S(1)}, f32[2,4,128,128]{3,2,1,0:T(8,128)S(1)}, u32[]{:S(2)}, u32[]{:S(2)}) collective-permute-start(f32[2,4,128,128]{3,2,1,0:T(8,128)S(1)} %get-tuple-element.12), channel_id=1, source_target_pairs={{0,2},{2,4},{4,6},{6,8},{8,10},{10,12},{12,14},{14,16},{16,18},{18... | collective-permute-start | bytes 1572872 | tf_op jit(solution)/shard_map/ppermute | solution.py:315
  5.1 2.4 %collective-permute-start.1 = (f32[2,2,128,128]{3,2,1,0:T(8,128)S(1)}, f32[2,2,128,128]{3,2,1,0:T(8,128)S(1)}, u32[]{:S(2)}, u32[]{:S(2)}) collective-permute-start(f32[2,2,128,128]{3,2,1,0:T(8,128)S(1)} %get-tuple-element.13), channel_id=1, source_target_pairs={{0,1},{1,0},{2,3},{3,2},{4,5},{5,4},{6,7},{7,6},{8,9},{9,8},{10,11... | collective-permute-start | bytes 786440 | tf_op jit(solution)/shard_map/ppermute | solution.py:324
  7.5 1.6 %collective-permute-start.2 = (f32[2,2,128,128]{3,2,1,0:T(8,128)S(1)}, f32[2,2,128,128]{3,2,1,0:T(8,128)S(1)}, u32[]{:S(2)}, u32[]{:S(2)}) collective-permute-start(f32[2,2,128,128]{3,2,1,0:T(8,128)S(1)} %get-tuple-element.14), channel_id=1, source_target_pairs={{0,3},{1,2},{2,5},{3,4},{4,7},{5,6},{6,9},{7,8},{8,11},{9,10},{10,... | collective-permute-start | bytes 786440 | tf_op jit(solution)/shard_map/ppermute | solution.py:325
  9.1 7.2 %collective-permute-done.1.refs_5_ = f32[2,2,128,128]{3,2,1,0:T(8,128)S(1)} collective-permute-done((f32[2,2,128,128]{3,2,1,0:T(8,128)S(1)}, f32[2,2,128,128]{3,2,1,0:T(8,128)S(1)}, u32[]{:S(2)}, u32[]{:S(2)}) %collective-permute-start.1) | collective-permute-done | bytes 262176 | tf_op jit(solution)/shard_map/ppermute | solution.py:324
  16.3 3.6 %collective-permute-done.2.refs_6_ = f32[2,2,128,128]{3,2,1,0:T(8,128)S(1)} collective-permute-done((f32[2,2,128,128]{3,2,1,0:T(8,128)S(1)}, f32[2,2,128,128]{3,2,1,0:T(8,128)S(1)}, u32[]{:S(2)}, u32[]{:S(2)}) %collective-permute-start.2) | collective-permute-done | bytes 262176 | tf_op jit(solution)/shard_map/ppermute | solution.py:325
  19.8 0.0 collective-permute-done.refs_4_
  19.8 0.0 copy-done.2
  19.8 0.0 copy-done.4
  19.9 0.0 copy-done.6
  19.9 0.0 copy-done.8
  19.9 0.0 copy-done.7
  19.9 5.3 %sweep.1 = (f32[2,2,4,128,128]{4,3,2,1,0:T(8,128)S(1)}, f32[256,128]{1,0:T(8,128)}, f32[2,4,64,128]{3,2,1,0:T(8,128)S(1)}, f32[2,4,64,128]{3,2,1,0:T(8,128)S(1)}) custom-call(f32[4,4]{1,0:T(4,128)S(1)} %copy-done.8, f32[8,4]{1,0:T(8,128)S(1)} %copy-done.7, f32[1,2,2,4,128,128]{5,4,3,2,1,0:T(8,128)S(1)} %copy-done, f32[2,4,128,128]{3,2,1,0:T(8,128)S(1)} %copy-done.1, ...), custom_call_target="tpu_custom_call" | custom-call | tf_op jit(solution)/shard_map/sweep/pallas_call | solution.py:335
  25.1 5.4 %all-to-all-start = ((f32[32,8,128]{2,1,0:T(8,128)}), f32[32,8,128]{2,1,0:T(8,128)S(1)}, u32[]{:S(2)}, u32[]{:S(2)}) async-start(f32[32,8,128]{2,1,0:T(8,128)} %bitcast), calls=%async_computation | async-start | bytes 262144 | tf_op jit(solution)/shard_map/all_to_all | solution.py:348
  30.6 1.8 %collective-permute-start.3 = (f32[2,4,64,128]{3,2,1,0:T(8,128)S(1)}, f32[2,4,64,128]{3,2,1,0:T(8,128)S(1)}, u32[]{:S(2)}, u32[]{:S(2)}) collective-permute-start(f32[2,4,64,128]{3,2,1,0:T(8,128)S(1)} %get-tuple-element.18), channel_id=1, source_target_pairs={{0,1},{1,0},{2,3},{3,2},{4,5},{5,4},{6,7},{7,6},{8,9},{9,8},{10,11... | collective-permute-start | bytes 786440 | tf_op jit(solution)/shard_map/ppermute | solution.py:350
  32.4 6.8 %all-to-all-done.pieces = f32[32,8,128]{2,1,0:T(8,128)S(1)} async-done(((f32[32,8,128]{2,1,0:T(8,128)}), f32[32,8,128]{2,1,0:T(8,128)S(1)}, u32[]{:S(2)}, u32[]{:S(2)}) %all-to-all-start) | async-done | bytes 131104 | tf_op jit(solution)/shard_map/all_to_all | solution.py:348
  39.2 0.7 %chain.1 = f32[32,8,128]{2,1,0:T(8,128)} custom-call(f32[32,8,128]{2,1,0:T(8,128)S(1)} %all-to-all-done.pieces, f32[8,128]{1,0:T(8,128)S(1)} %constant_dynamic-slice_fusion.factor), custom_call_target="tpu_custom_call" | custom-call | tf_op jit(solution)/shard_map/chain/pallas_call | solution.py:355
  39.9 2.7 %all-to-all-start.1 = ((f32[32,8,128]{2,1,0:T(8,128)}), f32[32,8,128]{2,1,0:T(8,128)S(1)}, u32[]{:S(2)}, u32[]{:S(2)}) async-start(f32[32,8,128]{2,1,0:T(8,128)} %chain.1), calls=%async_computation.1 | async-start | bytes 262144 | tf_op jit(solution)/shard_map/all_to_all | solution.py:363
  42.6 0.0 collective-permute-done.3.refs_0_
  42.6 8.6 %all-to-all-done.1 = f32[32,8,128]{2,1,0:T(8,128)S(1)} async-done(((f32[32,8,128]{2,1,0:T(8,128)}), f32[32,8,128]{2,1,0:T(8,128)S(1)}, u32[]{:S(2)}, u32[]{:S(2)}) %all-to-all-start.1) | async-done | bytes 131104 | tf_op jit(solution)/shard_map/all_to_all | solution.py:363
  51.2 3.0 %finish.1 = f32[1,2,2,4,128,128]{5,4,3,2,1,0:T(8,128)} custom-call(f32[8,4]{1,0:T(8,128)S(1)} %copy-done.7, f32[256,128]{1,0:T(8,128)S(1)} %bitcast.2, f32[2,2,4,128,128]{4,3,2,1,0:T(8,128)S(1)} %get-tuple-element.16.swept, f32[2,4,64,128]{3,2,1,0:T(8,128)S(1)} %get-tuple-element.17.keep, f32[2,4,64,128]{3,2,1,0:T(8,128)S(1)} %collective-permute-done.3.refs_0_, ...), custom_call_target="tpu_custom_call" | custom-call | tf_op jit(solution)/shard_map/finish/pallas_call | solution.py:365
  (11 shorter events, 0.0 us)
Async XLA Ops:
  0.0 1.2 %copy-start = (f32[1,2,2,4,128,128]{5,4,3,2,1,0:T(8,128)S(1)}, f32[1,2,2,4,128,128]{5,4,3,2,1,0:T(8,128)}, u32[]{:S(2)}) copy-start(f32[1,2,2,4,128,128]{5,4,3,2,1,0:T(8,128)} %refs_2_.1) | copy-start | bytes 3145732
  1.2 1.0 %copy-start.1 = (f32[2,4,128,128]{3,2,1,0:T(8,128)S(1)}, f32[2,4,128,128]{3,2,1,0:T(8,128)}, u32[]{:S(2)}) copy-start(f32[2,4,128,128]{3,2,1,0:T(8,128)} %refs_3_.2) | copy-start | bytes 1572868
  2.3 17.6 %copy-start.2 = (f32[256,128]{1,0:T(8,128)S(1)}, f32[256,128]{1,0:T(8,128)}, u32[]{:S(2)}) copy-start(f32[256,128]{1,0:T(8,128)} %constant.48.clone.refs_9_.refs_3_) | copy-start | bytes 393220
  2.3 17.6 %copy-start.4 = (bf16[2,256,128]{2,1,0:T(8,128)(2,1)S(1)}, bf16[2,256,128]{2,1,0:T(8,128)(2,1)}, u32[]{:S(2)}) copy-start(bf16[2,256,128]{2,1,0:T(8,128)(2,1)} %constant.55.refs_8_) | copy-start | bytes 393220
  2.3 17.6 %copy-start.6 = (bf16[2,64,128]{2,1,0:T(8,128)(2,1)S(1)}, bf16[2,64,128]{2,1,0:T(8,128)(2,1)}, u32[]{:S(2)}) copy-start(bf16[2,64,128]{2,1,0:T(8,128)(2,1)} %constant.52.refs_7_) | copy-start | bytes 98308
  2.3 17.6 %copy-start.8 = (f32[4,4]{1,0:T(4,128)S(1)}, f32[4,4]{1,0:T(4,128)}, u32[]{:S(2)}) copy-start(f32[4,4]{1,0:T(4,128)} %constant.38.clone.refs_0_) | copy-start | bytes 196
  2.7 17.2 %copy-start.7 = (f32[8,4]{1,0:T(8,128)S(1)}, f32[8,4]{1,0:T(8,128)}, u32[]{:S(2)}) copy-start(f32[8,4]{1,0:T(8,128)} %constant.39.clone.refs_1_.interp_z) | copy-start | bytes 388
  2.7 17.2 %collective-permute-start = (f32[2,4,128,128]{3,2,1,0:T(8,128)S(1)}, f32[2,4,128,128]{3,2,1,0:T(8,128)S(1)}, u32[]{:S(2)}, u32[]{:S(2)}) collective-permute-start(f32[2,4,128,128]{3,2,1,0:T(8,128)S(1)} %get-tuple-element.12), channel_id=1, source_target_pairs={{0,2},{2,4},{4,6},{6,8},{8,10},{10,12},{12,14},{14,16},{16,18},{18... | collective-permute-start | bytes 1572872 | tf_op jit(solution)/shard_map/ppermute | solution.py:315
  5.1 11.1 %collective-permute-start.1 = (f32[2,2,128,128]{3,2,1,0:T(8,128)S(1)}, f32[2,2,128,128]{3,2,1,0:T(8,128)S(1)}, u32[]{:S(2)}, u32[]{:S(2)}) collective-permute-start(f32[2,2,128,128]{3,2,1,0:T(8,128)S(1)} %get-tuple-element.13), channel_id=1, source_target_pairs={{0,1},{1,0},{2,3},{3,2},{4,5},{5,4},{6,7},{7,6},{8,9},{9,8},{10,11... | collective-permute-start | bytes 786440 | tf_op jit(solution)/shard_map/ppermute | solution.py:324
  7.5 12.3 %collective-permute-start.2 = (f32[2,2,128,128]{3,2,1,0:T(8,128)S(1)}, f32[2,2,128,128]{3,2,1,0:T(8,128)S(1)}, u32[]{:S(2)}, u32[]{:S(2)}) collective-permute-start(f32[2,2,128,128]{3,2,1,0:T(8,128)S(1)} %get-tuple-element.14), channel_id=1, source_target_pairs={{0,3},{1,2},{2,5},{3,4},{4,7},{5,6},{6,9},{7,8},{8,11},{9,10},{10,... | collective-permute-start | bytes 786440 | tf_op jit(solution)/shard_map/ppermute | solution.py:325
  25.1 14.0 %all-to-all-start = ((f32[32,8,128]{2,1,0:T(8,128)}), f32[32,8,128]{2,1,0:T(8,128)S(1)}, u32[]{:S(2)}, u32[]{:S(2)}) async-start(f32[32,8,128]{2,1,0:T(8,128)} %bitcast), calls=%async_computation | async-start | bytes 262144 | tf_op jit(solution)/shard_map/all_to_all | solution.py:348
  30.6 12.0 %collective-permute-start.3 = (f32[2,4,64,128]{3,2,1,0:T(8,128)S(1)}, f32[2,4,64,128]{3,2,1,0:T(8,128)S(1)}, u32[]{:S(2)}, u32[]{:S(2)}) collective-permute-start(f32[2,4,64,128]{3,2,1,0:T(8,128)S(1)} %get-tuple-element.18), channel_id=1, source_target_pairs={{0,1},{1,0},{2,3},{3,2},{4,5},{5,4},{6,7},{7,6},{8,9},{9,8},{10,11... | collective-permute-start | bytes 786440 | tf_op jit(solution)/shard_map/ppermute | solution.py:350
  39.9 11.3 %copy-start.3 = (bf16[2,128,256]{2,1,0:T(8,128)(2,1)S(1)}, bf16[2,128,256]{2,1,0:T(8,128)(2,1)}, u32[]{:S(2)}) copy-start(bf16[2,128,256]{2,1,0:T(8,128)(2,1)} %constant.61.refs_2_) | copy-start | bytes 393220
  39.9 11.3 %copy-start.5 = (bf16[2,128,64]{2,1,0:T(8,128)(2,1)S(1)}, bf16[2,128,64]{2,1,0:T(8,128)(2,1)}, u32[]{:S(2)}) copy-start(bf16[2,128,64]{2,1,0:T(8,128)(2,1)} %constant.58.refs_1_) | copy-start | bytes 98308
  39.9 11.3 %all-to-all-start.1 = ((f32[32,8,128]{2,1,0:T(8,128)}), f32[32,8,128]{2,1,0:T(8,128)S(1)}, u32[]{:S(2)}, u32[]{:S(2)}) async-start(f32[32,8,128]{2,1,0:T(8,128)} %chain.1), calls=%async_computation.1 | async-start | bytes 262144 | tf_op jit(solution)/shard_map/all_to_all | solution.py:363
